TPU v7x, 256 devices: a whole 4x4x8 slice. The times are simulated.
256 devices in a mesh: seq: 32 (over y, z), head: 8 (over x, core).
Axes of the slice: x: 4, y: 4, z: 8, core: 2. Of those that a mesh axis runs over, the one named last changes fastest.
Arguments:
- inputs: bfloat16 [8192, 8192], P('seq'), may hold values from -6 to 6
- w_value: bfloat16 [8192, 4096], P('seq', 'head'), may hold values from -0.0625 to 0.0625
- log_decay: float32 [8192, 64], P('seq', 'head'), may hold values from -1 to 0
- b_proj: bfloat16 [8192, 128], P('seq'), may hold values from -0.5 to 0.5
- c_proj: bfloat16 [8192, 128], P('seq'), may hold values from -0.5 to 0.5
- grad_out: bfloat16 [8192, 4096], P('seq', 'head'), may hold values from -6 to 6
Outputs:
- grad_input: bfloat16 [8192, 8192], P('seq', 'head')
- grad_weight: float32 [8192, 4096], P('seq', 'head')
- grad_b: float32 [8192, 128], P('seq')
- grad_c: float32 [8192, 128], P('seq')
All inputs are finite; a program needn't handle non-finite values.
Results may differ from a plain program's by a relative error of at most 0.027.
Values may be sent and summed in bfloat16 or wider, within the bound.
A program may use at most 128 MiB of HBM per device.

v0:
```python
import jax
import jax.numpy as jnp
from jax import lax
from jax.sharding import PartitionSpec as P

SPAN = 256
HIGH = lax.Precision.HIGHEST


def carried_in(array, axis, combine, identity, reverse):
    length, index = (lax.axis_size(axis), lax.axis_index(axis))
    everything = jax.tree.map(
        lambda part, kind: lax.all_gather(part.astype(kind), axis),
        array,
        (jnp.bfloat16, jnp.bfloat16),
    )
    start = jax.tree.map(
        lambda part, zero: jnp.broadcast_to(jnp.asarray(zero, part.dtype), part.shape),
        array,
        identity,
    )

    def lap(k, before):
        at = length - 1 - k if reverse else k
        reached = at > index if reverse else at < index
        new = combine(
            before, jax.tree.map(lambda part, own: part[at].astype(own.dtype), everything, array)
        )
        return jax.tree.map(lambda a, b: jnp.where(reached, a, b), new, before)

    return lax.fori_loop(0, length, lap, start)


def link(earlier, later):
    return (earlier[0] * later[0], later[0][:, None, None] * earlier[1] + later[1])


def advance_once(carried, item):
    decay, local = item
    return (decay[:, None, None] * carried + local, carried)


def per_device(inputs, w_value, log_decay, b_proj, c_proj, grad_out):
    steps = inputs.shape[0]
    heads = log_decay.shape[1]
    columns = grad_out.shape[1]
    depth = columns // heads
    states = b_proj.shape[1]
    blocks = steps // SPAN
    w_full = lax.all_gather(w_value, "seq", axis=0, tiled=True)
    values = jnp.dot(inputs, w_full, preferred_element_type=jnp.float32).astype(jnp.bfloat16)
    xs = values.astype(jnp.float32).reshape(blocks, SPAN, heads, depth)
    dys = grad_out.astype(jnp.float32).reshape(blocks, SPAN, heads, depth)
    bs = b_proj.astype(jnp.float32).reshape(blocks, SPAN, states)
    cs = c_proj.astype(jnp.float32).reshape(blocks, SPAN, states)
    cum_log = jnp.cumsum(log_decay.reshape(blocks, SPAN, heads), axis=1)
    totals = cum_log[:, -1]
    grow = jnp.exp(cum_log)
    shrink = jnp.exp(totals[:, None] - cum_log)
    cum_heads = jnp.swapaxes(cum_log, 1, 2)
    rows = lax.broadcasted_iota(jnp.int32, (SPAN, SPAN), 0)
    cols = lax.broadcasted_iota(jnp.int32, (SPAN, SPAN), 1)
    lower = (rows >= cols)[None, None]
    diff = cum_heads[:, :, :, None] - cum_heads[:, :, None, :]
    decay_mat = jnp.exp(jnp.where(lower, diff, -jnp.inf))
    cross = jnp.einsum("kthp,kjhp->khtj", dys, xs, precision=HIGH)
    mixed = decay_mat * cross
    scores = jnp.einsum("ktn,kjn->ktj", cs, bs, precision=HIGH)
    span_decay = jnp.exp(totals)
    dev_decay = jnp.exp(jnp.sum(totals, axis=0))
    zero_state = jnp.zeros((heads, depth, states), jnp.float32)
    identity_matrix = (jnp.ones_like(dev_decay), zero_state)
    local_end = jnp.einsum("kjhp,kjh,kjn->khpn", xs, shrink, bs, precision=HIGH)
    dev_state, before = lax.scan(advance_once, zero_state, (span_decay, local_end))
    incoming = carried_in((dev_decay, dev_state), "seq", link, identity_matrix, False)[1]
    lead = jnp.exp(jnp.cumsum(totals, axis=0) - totals)
    state_in = before + lead[:, :, None, None] * incoming[None]
    grad_c = jnp.einsum("kthp,khpn,kth->ktn", dys, state_in, grow, precision=HIGH)
    grad_c = grad_c + jnp.einsum("khtj,kjn->ktn", mixed, bs, precision=HIGH)
    local_back = jnp.einsum("kthp,kth,ktn->khpn", dys, grow, cs, precision=HIGH)
    dev_back, after = lax.scan(advance_once, zero_state, (span_decay, local_back), reverse=True)
    incoming_back = carried_in((dev_decay, dev_back), "seq", link, identity_matrix, True)[1]
    trail = jnp.exp(jnp.sum(totals, axis=0)[None] - jnp.cumsum(totals, axis=0))
    grad_in = after + trail[:, :, None, None] * incoming_back[None]
    grad_vals = jnp.einsum("khst,kst,kshp->kthp", decay_mat, scores, dys, precision=HIGH)
    grad_vals = grad_vals + jnp.einsum("khpn,ktn,kth->kthp", grad_in, bs, shrink, precision=HIGH)
    grad_b = jnp.einsum("khst,ksn->ktn", mixed, cs, precision=HIGH)
    grad_b = grad_b + jnp.einsum("kthp,khpn,kth->ktn", xs, grad_in, shrink, precision=HIGH)
    grad_values = grad_vals.reshape(steps, columns).astype(jnp.bfloat16)
    grad_b, grad_c = (
        lax.psum(grad_b.reshape(steps, states).astype(jnp.bfloat16), "head").astype(jnp.float32),
        lax.psum(grad_c.reshape(steps, states).astype(jnp.bfloat16), "head").astype(jnp.float32),
    )
    term = lax.dot_general(
        grad_values, w_full, (((1,), (1,)), ((), ())), preferred_element_type=jnp.float32
    )
    grad_input = lax.psum_scatter(
        term.astype(jnp.bfloat16), "head", scatter_dimension=1, tiled=True
    )
    grad_weight = lax.psum_scatter(
        lax.dot_general(
            inputs, grad_values, (((0,), (0,)), ((), ())), preferred_element_type=jnp.float32
        ).astype(jnp.bfloat16),
        "seq",
        scatter_dimension=0,
        tiled=True,
    ).astype(jnp.float32)
    return (grad_input, grad_weight, grad_b, grad_c)


def solution(mesh):
    placed = (
        P("seq", None),
        P("seq", "head"),
        P("seq", "head"),
        P("seq", None),
        P("seq", None),
        P("seq", "head"),
    )
    return jax.shard_map(
        per_device,
        mesh=mesh,
        in_specs=placed,
        out_specs=(P("seq", "head"), P("seq", "head"), P("seq", None), P("seq", None)),
        check_vma=False,
    )
```

profile of v0, /device:TPU:8, one launch (start us, length us, event | category | flops | bytes accessed | tf_op | source)
XLA Modules:
  0.0 655.9 jit_solution(10136107935495648219)
XLA Ops:
  8.0 1.3 reduce-window.6
  9.4 1.1 copy.32
  10.8 1.9 fusion.18
  13.0 41.5 %all-gather = bf16[32,1,8]{2,1,0:T(2,128)(2,1)S(1)} all-gather(bf16[1,1,8]{2,1,0:T(2,128)(2,1)S(1)} %copy.34), channel_id=2, replica_groups=mesh['seq'=32,'head'=8] {'seq'}, dimensions={0}, use_global_device_ids=true | all-gather | bytes 528 | tf_op jit(solution)/shard_map/all_gather | solution.py:13
  54.6 1.0 fusion.43
  55.7 54.8 %all-gather.7.cloned.1.call-done = bf16[8192,512]{1,0:T(8,128)(2,1)} async-done(((bf16[256,512]{1,0:T(8,128)(2,1)}), bf16[8192,512]{1,0:T(8,128)(2,1)}) %all-gather.7.cloned.1.call-update) | async-done | bytes 8388624 | tf_op jit(solution)/shard_map/all_gather | solution.py:50
  110.5 7.0 %convolution_convert_fusion.2 = bf16[256,512]{1,0:T(8,128)(2,1)S(1)} fusion(bf16[256,8192]{1,0:T(8,128)(2,1)} %param.10, bf16[8192,512]{1,0:T(8,128)(2,1)} %all-gather.7.cloned.1.call-done), kind=kOutput, calls=%fused_computation.21 | convolution fusion | flops 2147614720 | bytes 12845056 | tf_op jit(solution)/shard_map/dot_general | solution.py:51
  117.6 1.1 fusion.19
  118.7 73.8 %all-gather.9.cloned.1.call-done = bf16[256,64,128]{2,1,0:T(8,128)(2,1)} async-done(((bf16[8,64,128]{2,1,0:T(8,128)(2,1)}), bf16[256,64,128]{2,1,0:T(8,128)(2,1)}) %all-gather.9.cloned.1.call-update) | async-done | bytes 4194320 | tf_op jit(solution)/shard_map/all_gather | solution.py:13
  192.5 34.1 %while.40 = (s32[]{:T(128)}, f32[8,64,128]{2,1,0:T(8,128)S(1)}, s32[]{:T(128)}, bf16[32,8]{1,0:T(8,128)(2,1)S(1)}, bf16[32,8,64,128]{3,2,1,0:T(8,128)(2,1)}, /*index=5*/s32[]{:T(128)}, s32[]{:T(128)}, s32[]{:T(128)}, s32[]{:T(128)}) while((s32[]{:T(128)}, f32[8,64,128]{2,1,0:T(8,128)S(1)}, s32[]{:T(128)}, ...), condition=%wide.region_3.4_spmd.clone, body=%wide.region_2.3_spmd.clone.sunk | while | flops 327696 | bytes 655607 | solution.py:31
  197.9 1.0 fusion.61
  198.9 1.0 fusion.61
  200.0 1.0 fusion.61
  201.1 1.0 fusion.61
  202.1 1.0 fusion.61
  205.3 1.0 fusion.61
  206.4 1.0 fusion.61
  216.0 1.0 fusion.61
  227.1 1.6 fusion.15
  228.7 1.0 convolution_bitcast_fusion.2
  231.4 43.4 %all-gather.11.cloned.1.call-done = bf16[256,64,128]{2,1,0:T(8,128)(2,1)} async-done(((bf16[8,64,128]{2,1,0:T(8,128)(2,1)}), bf16[256,64,128]{2,1,0:T(8,128)(2,1)}) %all-gather.11.cloned.1.call-update) | async-done | bytes 4194320 | tf_op jit(solution)/shard_map/all_gather | solution.py:13
  274.8 33.7 %while.41 = (s32[]{:T(128)}, f32[8,64,128]{2,1,0:T(8,128)S(1)}, s32[]{:T(128)}, bf16[32,8]{1,0:T(8,128)(2,1)S(1)}, bf16[32,8,64,128]{3,2,1,0:T(8,128)(2,1)}, /*index=5*/s32[]{:T(128)}, s32[]{:T(128)}) while((s32[]{:T(128)}, f32[8,64,128]{2,1,0:T(8,128)S(1)}, s32[]{:T(128)}, bf16[32,8]{1,0:T(8,128)(2,1)S(1)}, ...), condition=%wide.region_9.10_spmd.clone, body=%wide.region_8.9_spmd.clone.sunk | while | flops 327692 | bytes 655545 | solution.py:31
  308.5 1.0 convolution_bitcast_fusion.1
  309.5 1.0 fusion.21
  310.6 7.8 %fusion.2 = bf16[8192,512]{0,1:T(8,128)(2,1)} fusion(bf16[256,512]{0,1:T(8,128)(2,1)S(1)} %bitcast.122, bf16[256,8192]{1,0:T(8,128)(2,1)} %param.10), kind=kOutput, calls=%fused_computation.7 | convolution fusion | flops 2151677952 | bytes 12845056 | tf_op jit(solution)/shard_map/dot_general | solution.py:101
  318.6 7.8 %convolution_convert_fusion.1 = bf16[256,8192]{1,0:T(8,128)(2,1)} fusion(bf16[256,512]{0,1:T(8,128)(2,1)S(1)} %bitcast.123, bf16[8192,512]{1,0:T(8,128)(2,1)} %all-gather.7.cloned.1.call-done), kind=kOutput, calls=%fused_computation.8 | convolution fusion | flops 2149580800 | bytes 12845056 | tf_op jit(solution)/shard_map/dot_general | solution.py:94
  326.4 47.2 %all-reduce.3.cloned.1.call-done = (bf16[256,128]{1,0:T(8,128)(2,1)}, bf16[256,128]{1,0:T(8,128)(2,1)}) async-done(((bf16[256,128]{1,0:T(8,128)(2,1)}, bf16[256,128]{1,0:T(8,128)(2,1)}), (bf16[256,128]{1,0:T(8,128)(2,1)}, bf16[256,128]{1,0:T(8,128)(2,1)})) %all-reduce.3.cloned.1.call-update) | async-done | bytes 131088 | tf_op jit(solution)/shard_map/psum | solution.py:91
  373.6 1.5 convert_element_type.131
  375.1 1.5 convert_element_type.135
  376.6 229.8 %reduce-scatter.5.cloned.1.call-done = bf16[256,512]{0,1:T(8,128)(2,1)} async-done(((bf16[8192,512]{0,1:T(8,128)(2,1)}), bf16[256,512]{0,1:T(8,128)(2,1)}) %reduce-scatter.5.cloned.1.call-update) | async-done | bytes 262160 | tf_op jit(solution)/shard_map/reduce_scatter | solution.py:100
  606.4 1.9 copy.39
  608.3 40.7 %reduce-scatter.3.cloned.1.call-done = bf16[256,1024]{1,0:T(8,128)(2,1)} async-done(((bf16[256,8192]{1,0:T(8,128)(2,1)}), bf16[256,1024]{1,0:T(8,128)(2,1)}) %reduce-scatter.3.cloned.1.call-update) | async-done | bytes 524304 | tf_op jit(solution)/shard_map/reduce_scatter | solution.py:97
  (154 shorter events, 61.6 us)
Async XLA Ops:
  7.2 47.5 %copy-start = (bf16[256,128]{1,0:T(8,128)(2,1)S(1)}, bf16[256,128]{1,0:T(8,128)(2,1)}, u32[]{:S(2)}) copy-start(bf16[256,128]{1,0:T(8,128)(2,1)} %param.13) | copy-start | bytes 196612
  7.2 103.3 %all-gather.7.cloned.1.call-start = ((), (), s32[]{:S(2)}) async-start(), calls=%async_computation.2 | async-start | bytes 8650752 | tf_op jit(solution)/shard_map/all_gather | solution.py:50
  7.9 184.6 %all-gather.9.cloned.1.call-start = ((), (), s32[]{:S(2)}) async-start(), calls=%async_computation.5 | async-start | bytes 4325376 | tf_op jit(solution)/shard_map/all_gather | solution.py:13
  12.7 262.1 %all-gather.11.cloned.1.call-start = ((), (), s32[]{:S(2)}) async-start(), calls=%async_computation.6 | async-start | bytes 4325376 | tf_op jit(solution)/shard_map/all_gather | solution.py:13
  118.7 254.9 %all-reduce.3.cloned.1.call-start = ((), (), s32[]{:S(2)}) async-start(), calls=%async_computation.7 | async-start | bytes 262144 | tf_op jit(solution)/shard_map/psum | solution.py:91
  226.6 3.8 copy-start.1
  310.5 295.9 %reduce-scatter.5.cloned.1.call-start = ((), (), s32[]{:S(2)}) async-start(), calls=%async_computation.4 | async-start | bytes 8650752 | tf_op jit(solution)/shard_map/reduce_scatter | solution.py:100
  318.4 330.7 %reduce-scatter.3.cloned.1.call-start = ((), (), s32[]{:S(2)}) async-start(), calls=%async_computation.3 | async-start | bytes 4718592 | tf_op jit(solution)/shard_map/reduce_scatter | solution.py:97
Sparse Core Ops, SparseCore 0:
  10.6 99.8 all-gather.6
  113.6 78.8 all-gather.8
  195.7 79.0 all-gather.10
  310.7 62.9 all-reduce.2
  378.0 228.3 reduce-scatter.4
  609.4 39.6 reduce-scatter.2
where the time goes:
time: 657 us; the launch traced here: 656 us
  waiting for transfers between devices  491 us (75%)
  other arithmetic  70.2 us (11%)
  blocking collectives  41.5 us (6%)
  matrix products  33.2 us (5%)
  between operations  14.3 us (2%)
    reduce_scatter x1, waiting for transfers between devices, per_device(): lax.psum_scatter(lax.dot_general(inputs, grad_values, (((0,), (0,)), ((),...  230 us
    all_gather x2, waiting for transfers between devices, carried_in(): lax.all_gather(part.astype(kind), axis)  117 us
    select_n x64, other arithmetic, lap(): return jax.tree.map(lambda a, b: jnp.where(reached, a, b), new, before)  64.8 us
    all_gather x1, waiting for transfers between devices, per_device(): w_full = lax.all_gather(w_value, 'seq', axis=0, tiled=True)  54.8 us
    psum x1, waiting for transfers between devices, per_device(): lax.psum(grad_b.reshape(steps, states).astype(jnp.bfloat16), 'head')  47.2 us
    all_gather x1, blocking collectives, carried_in(): lax.all_gather(part.astype(kind), axis)  41.5 us
    reduce_scatter x1, waiting for transfers between devices, per_device(): lax.psum_scatter(term.astype(jnp.bfloat16), 'head', scatter_dimension=1,...  40.7 us
  transfers between devices with their start and end apart: 6, of which 6 were waited for; matrix products, arithmetic and copies ran while one was open for 11% of the time, Pallas kernels for 0%

commit v1 on v0

--- a/solution.py
+++ b/solution.py
@@ -47,7 +47,10 @@
     depth = columns // heads
     states = b_proj.shape[1]
     blocks = steps // SPAN
-    w_full = lax.all_gather(w_value, "seq", axis=0, tiled=True)
+    size = lax.axis_size("seq")
+    pieces = jnp.stack([w_value for _ in range(size)])
+    pieces = lax.all_to_all(pieces, "seq", split_axis=0, concat_axis=0)
+    w_full = jnp.concatenate(pieces, axis=0)
     values = jnp.dot(inputs, w_full, preferred_element_type=jnp.float32).astype(jnp.bfloat16)
     xs = values.astype(jnp.float32).reshape(blocks, SPAN, heads, depth)
     dys = grad_out.astype(jnp.float32).reshape(blocks, SPAN, heads, depth)

time: 657 us -> 734 us (1.12)
  blocking collectives: 41.5 us -> 238 us
  waiting for transfers between devices: 491 us -> 358 us
  starting transfers between devices: 0.42 us -> 12.3 us
    all_gather x1, blocking collectives: 41.5 us -> 238 us  [carried_in(): lax.all_gather(part.astype(kind), axis)]
    all_gather x2, waiting for transfers between devices: 117 us -> 39.9 us  [carried_in(): lax.all_gather(part.astype(kind), axis)]
    all_gather x1 -> x0, waiting for transfers between devices: 54.8 us -> none  [per_device(): w_full = lax.all_gather(w_value, 'seq', axis=0, tiled=True)]
    all_to_all x0 -> x1, starting transfers between devices: none -> 11.9 us  [per_device(): pieces = lax.all_to_all(pieces, 'seq', split_axis=0, concat_axis=0)]
  transfers between devices with their start and end apart: 6 -> 6, of which waited for: 6 -> 4; matrix products, arithmetic and copies ran while one was open for 11% -> 9% of each run, Pallas kernels for 0% -> 0%
where the time goes in v1:
time: 734 us; the launch traced here: 733 us
  waiting for transfers between devices  358 us (49%)
  blocking collectives  238 us (32%)
  other arithmetic  69.5 us (9%)
  matrix products  31.6 us (4%)
  between operations  13.9 us (2%)
  starting transfers between devices  12.3 us (2%)
  local copies, waits for them, and re-layouts  7.77 us (1%)
    all_gather x1, blocking collectives, carried_in(): lax.all_gather(part.astype(kind), axis)  238 us
    reduce_scatter x1, waiting for transfers between devices, per_device(): lax.psum_scatter(lax.dot_general(inputs, grad_values, (((0,), (0,)), ((),...  230 us
    select_n x64, other arithmetic, lap(): return jax.tree.map(lambda a, b: jnp.where(reached, a, b), new, before)  64.9 us
    psum x1, waiting for transfers between devices, per_device(): lax.psum(grad_b.reshape(steps, states).astype(jnp.bfloat16), 'head')  47.2 us
    reduce_scatter x1, waiting for transfers between devices, per_device(): lax.psum_scatter(term.astype(jnp.bfloat16), 'head', scatter_dimension=1,...  40.8 us
    all_gather x2, waiting for transfers between devices, carried_in(): lax.all_gather(part.astype(kind), axis)  39.9 us
  transfers between devices with their start and end apart: 6, of which 4 were waited for; matrix products, arithmetic and copies ran while one was open for 9% of the time, Pallas kernels for 0%

profile of v1, /device:TPU:8, one launch (start us, length us, event | category | flops | bytes accessed | tf_op | source)
XLA Modules:
  0.0 732.7 jit_solution(10546251889988314916)
XLA Ops:
  7.2 5.2 stack.2
  12.3 11.9 %all-to-all-start = ((bf16[32,256,512]{2,1,0:T(8,128)(2,1)}), bf16[32,256,512]{2,1,0:T(8,128)(2,1)}, u32[]{:S(2)}, u32[]{:S(2)}) async-start(bf16[32,256,512]{2,1,0:T(8,128)(2,1)} %stack.2), calls=%async_computation | async-start | bytes 16777216 | tf_op jit(solution)/shard_map/all_to_all | solution.py:52
  25.5 1.1 fusion.18
  26.8 237.6 %all-gather = bf16[32,1,8]{2,1,0:T(2,128)(2,1)S(1)} all-gather(bf16[1,1,8]{2,1,0:T(2,128)(2,1)S(1)} %copy.34), channel_id=2, replica_groups=mesh['seq'=32,'head'=8] {'seq'}, dimensions={0}, use_global_device_ids=true | all-gather | bytes 528 | tf_op jit(solution)/shard_map/all_gather | solution.py:13
  264.8 7.0 convolution_convert_fusion.2
  271.9 1.1 fusion.19
  273.1 34.2 %while.40 = (s32[]{:T(128)}, f32[8,64,128]{2,1,0:T(8,128)S(1)}, s32[]{:T(128)}, bf16[32,8]{1,0:T(8,128)(2,1)S(1)}, bf16[32,8,64,128]{3,2,1,0:T(8,128)(2,1)}, /*index=5*/s32[]{:T(128)}, s32[]{:T(128)}, s32[]{:T(128)}, s32[]{:T(128)}) while((s32[]{:T(128)}, f32[8,64,128]{2,1,0:T(8,128)S(1)}, s32[]{:T(128)}, ...), condition=%wide.region_3.4_spmd.clone, body=%wide.region_2.3_spmd.clone.sunk | while | flops 327696 | bytes 655607 | solution.py:31
  274.2 1.0 fusion.61
  275.3 1.0 fusion.61
  276.4 1.0 fusion.61
  277.4 1.0 fusion.61
  278.5 1.0 fusion.61
  282.8 1.0 fusion.61
  283.8 1.0 fusion.61
  289.2 1.0 fusion.61
  296.6 1.0 fusion.61
  299.8 1.0 fusion.61
  305.2 1.0 fusion.61
  307.7 1.6 fusion.15
  309.3 1.0 convolution_bitcast_fusion.2
  312.0 39.9 %all-gather.8.cloned.1.call-done = bf16[256,64,128]{2,1,0:T(8,128)(2,1)} async-done(((bf16[8,64,128]{2,1,0:T(8,128)(2,1)}), bf16[256,64,128]{2,1,0:T(8,128)(2,1)}) %all-gather.8.cloned.1.call-update) | async-done | bytes 4194320 | tf_op jit(solution)/shard_map/all_gather | solution.py:13
  351.9 33.7 %while.41 = (s32[]{:T(128)}, f32[8,64,128]{2,1,0:T(8,128)S(1)}, s32[]{:T(128)}, bf16[32,8]{1,0:T(8,128)(2,1)S(1)}, bf16[32,8,64,128]{3,2,1,0:T(8,128)(2,1)}, /*index=5*/s32[]{:T(128)}, s32[]{:T(128)}) while((s32[]{:T(128)}, f32[8,64,128]{2,1,0:T(8,128)S(1)}, s32[]{:T(128)}, bf16[32,8]{1,0:T(8,128)(2,1)S(1)}, ...), condition=%wide.region_9.10_spmd.clone, body=%wide.region_8.9_spmd.clone.sunk | while | flops 327692 | bytes 655545 | solution.py:31
  385.6 1.0 convolution_bitcast_fusion.1
  386.6 1.0 fusion.21
  387.9 7.8 %fusion.2 = bf16[8192,512]{0,1:T(8,128)(2,1)} fusion(bf16[256,512]{0,1:T(8,128)(2,1)S(1)} %bitcast.123, bf16[256,8192]{1,0:T(8,128)(2,1)} %param.10), kind=kOutput, calls=%fused_computation.7 | convolution fusion | flops 2151677952 | bytes 12845056 | tf_op jit(solution)/shard_map/dot_general | solution.py:104
  395.7 7.8 %convolution_convert_fusion.1 = bf16[256,8192]{1,0:T(8,128)(2,1)} fusion(bf16[256,512]{0,1:T(8,128)(2,1)S(1)} %bitcast.124, bf16[8192,512]{1,0:T(8,128)(2,1)} %bitcast.23), kind=kOutput, calls=%fused_computation.8 | convolution fusion | flops 2149580800 | bytes 12845056 | tf_op jit(solution)/shard_map/dot_general | solution.py:97
  403.5 47.2 %all-reduce.3.cloned.1.call-done = (bf16[256,128]{1,0:T(8,128)(2,1)}, bf16[256,128]{1,0:T(8,128)(2,1)}) async-done(((bf16[256,128]{1,0:T(8,128)(2,1)}, bf16[256,128]{1,0:T(8,128)(2,1)}), (bf16[256,128]{1,0:T(8,128)(2,1)}, bf16[256,128]{1,0:T(8,128)(2,1)})) %all-reduce.3.cloned.1.call-update) | async-done | bytes 131088 | tf_op jit(solution)/shard_map/psum | solution.py:94
  450.7 1.5 convert_element_type.132
  452.2 1.5 convert_element_type.136
  453.7 229.8 %reduce-scatter.5.cloned.1.call-done = bf16[256,512]{0,1:T(8,128)(2,1)} async-done(((bf16[8192,512]{0,1:T(8,128)(2,1)}), bf16[256,512]{0,1:T(8,128)(2,1)}) %reduce-scatter.5.cloned.1.call-update) | async-done | bytes 262160 | tf_op jit(solution)/shard_map/reduce_scatter | solution.py:103
  683.5 1.9 copy.39
  685.4 40.8 %reduce-scatter.3.cloned.1.call-done = bf16[256,1024]{1,0:T(8,128)(2,1)} async-done(((bf16[256,8192]{1,0:T(8,128)(2,1)}), bf16[256,1024]{1,0:T(8,128)(2,1)}) %reduce-scatter.3.cloned.1.call-update) | async-done | bytes 524304 | tf_op jit(solution)/shard_map/reduce_scatter | solution.py:100
  (158 shorter events, 58.8 us)
Async XLA Ops:
  7.2 257.5 %copy-start = (bf16[256,128]{1,0:T(8,128)(2,1)S(1)}, bf16[256,128]{1,0:T(8,128)(2,1)}, u32[]{:S(2)}) copy-start(bf16[256,128]{1,0:T(8,128)(2,1)} %param.13) | copy-start | bytes 196612
  12.3 12.0 %copy-start.3 = (f32[256,8]{0,1:T(8,128)S(1)}, f32[256,8]{0,1:T(8,128)}, u32[]{:S(2)}) copy-start(f32[256,8]{0,1:T(8,128)} %param.12) | copy-start | bytes 24580
  12.3 12.7 %copy-start.2 = (bf16[256,512]{1,0:T(8,128)(2,1)S(1)}, bf16[256,512]{1,0:T(8,128)(2,1)}, u32[]{:S(2)}) copy-start(bf16[256,512]{1,0:T(8,128)(2,1)} %param.15) | copy-start | bytes 786436
  12.3 13.2 %copy-start.1 = (bf16[256,128]{1,0:T(8,128)(2,1)S(1)}, bf16[256,128]{1,0:T(8,128)(2,1)}, u32[]{:S(2)}) copy-start(bf16[256,128]{1,0:T(8,128)(2,1)} %param.14) | copy-start | bytes 196612
  12.3 252.5 %all-to-all-start = ((bf16[32,256,512]{2,1,0:T(8,128)(2,1)}), bf16[32,256,512]{2,1,0:T(8,128)(2,1)}, u32[]{:S(2)}, u32[]{:S(2)}) async-start(bf16[32,256,512]{2,1,0:T(8,128)(2,1)} %stack.2), calls=%async_computation | async-start | bytes 16777216 | tf_op jit(solution)/shard_map/all_to_all | solution.py:52
  24.2 248.9 %all-gather.6.cloned.1.call-start = ((), (), s32[]{:S(2)}) async-start(), calls=%async_computation.5 | async-start | bytes 4325376 | tf_op jit(solution)/shard_map/all_gather | solution.py:13
  26.6 325.3 %all-gather.8.cloned.1.call-start = ((), (), s32[]{:S(2)}) async-start(), calls=%async_computation.6 | async-start | bytes 4325376 | tf_op jit(solution)/shard_map/all_gather | solution.py:13
  273.0 177.7 %all-reduce.3.cloned.1.call-start = ((), (), s32[]{:S(2)}) async-start(), calls=%async_computation.7 | async-start | bytes 262144 | tf_op jit(solution)/shard_map/psum | solution.py:94
  387.6 295.8 %reduce-scatter.5.cloned.1.call-start = ((), (), s32[]{:S(2)}) async-start(), calls=%async_computation.4 | async-start | bytes 8650752 | tf_op jit(solution)/shard_map/reduce_scatter | solution.py:103
  395.7 330.5 %reduce-scatter.3.cloned.1.call-start = ((), (), s32[]{:S(2)}) async-start(), calls=%async_computation.3 | async-start | bytes 4718592 | tf_op jit(solution)/shard_map/reduce_scatter | solution.py:100
Sparse Core Ops, SparseCore 0:
  28.2 141.5 all-gather.5
  273.2 78.6 all-gather.7
  387.8 62.9 all-reduce.2
  455.1 228.3 reduce-scatter.4
  686.5 39.6 reduce-scatter.2
